TPU v7x, 512 devices: a whole 4x4x16 slice. The times are simulated.
512 devices in a mesh: rows: 64 (over y, z), cols: 8 (over x, core).
Axes of the slice: x: 4, y: 4, z: 16, core: 2. Of those that a mesh axis runs over, the one named last changes fastest.
Arguments:
- vectors: float32 [512, 131072], P(None, ('rows', 'cols')), may hold values from -80 to 80
- offsets: int32 [16, 131072], P(None, ('rows', 'cols')), may hold values from -256 to 256, as said below
- counts: int32 [131072], P(('rows', 'cols')), may hold values from 8 to 16
- labels: int32 [2, 131072], P(None, ('rows', 'cols')), may hold values from 0 to 1
- cosines: float32 [16, 131072], P(None, ('rows', 'cols')), may hold values from -1 to 1
- distances: float32 [16, 131072], P(None, ('rows', 'cols')), may hold values from 1 to 3
Outputs:
- basis: float32 [512, 131072], P('cols', 'rows')
Inputs may be any that keep to these rules, and one draw needn't show every extreme that they name: `offsets`: each offset is nonzero and at most 256 in magnitude; both -256 and 256 occur. Offsets follow a lattice: small in-row steps, steps near half of 256, and steps near 256.
All inputs are finite; a program needn't handle non-finite values.
Results may differ from a plain program's by a relative error of at most 0.00012.
Values sent between devices are 32-bit elements; how exact they have to be, the bound alone decides.
No kernel may reach another device: no remote copies, remote signals or barrier semaphores. Data moves between devices by JAX's collectives and lax.ppermute only.
A program may use at most 64 MiB of HBM per device.

v0:
```python
import jax
import jax.numpy as jnp
from jax import lax
from jax.sharding import PartitionSpec as P

REACH = 256
PI_BOND = -1.0
SIGMA_BOND = 0.178
DECAY_LENGTH = 0.319
LAYER_GAP = 2.36
SITE_MASS = 0.4
LAYER_BIAS = 0.25


def extended_2(block, sides, width):
    for axis, dim in sides:
        count = lax.axis_size(axis)
        forward = [(i, i + 1) for i in range(count - 1)]
        forward.append((count - 1, 0))
        backward = [(target, source) for source, target in forward]
        low = lax.ppermute(
            lax.slice_in_dim(block, block.shape[dim] - width, None, axis=dim), axis, forward
        )
        high = lax.ppermute(lax.slice_in_dim(block, 0, width, axis=dim), axis, backward)
        block = jnp.concatenate([low, block, high], axis=dim)
    return block


def spread(value, axis, source):
    kept = jnp.where(lax.axis_index(axis) == source, value, 0).astype(value.dtype)
    return lax.psum(kept, axis)


def hop_table(cosines, distances, counts):
    square = cosines * cosines
    bond_value = PI_BOND * jnp.exp(-(distances - 1.0) / DECAY_LENGTH) * (1.0 - square)
    bond_value = bond_value + SIGMA_BOND * jnp.exp(-(distances - LAYER_GAP) / DECAY_LENGTH) * square
    slot_index = lax.broadcasted_iota(jnp.int32, cosines.shape, 0)
    return jnp.where(slot_index < counts[None, :], bond_value, jnp.zeros_like(bond_value))


def onsite_of(labels):
    sublattice = (2 * labels[0] - 1).astype(jnp.float32)
    layer_sign = (2 * labels[1] - 1).astype(jnp.float32)
    return SITE_MASS * sublattice + LAYER_BIAS * layer_sign


def apply_local(extended, hopping, offsets, onsite):
    atom_count = hopping.shape[1]
    middle = extended[:, REACH : REACH + atom_count]
    column = jnp.arange(atom_count, dtype=jnp.int32) + REACH

    def advance(slot_index, running):
        target = column + offsets[slot_index]
        return running + hopping[slot_index][None, :] * jnp.take(extended, target, axis=1)

    return lax.fori_loop(0, hopping.shape[0], advance, onsite[None, :] * middle)


def regroup(source):
    return lax.all_to_all(source, "cols", split_axis=0, concat_axis=1, tiled=True)


def on_device(vectors, offsets, counts, labels, cosines, distances):
    highest = lax.Precision.HIGHEST
    hopping = hop_table(cosines, distances, counts)
    onsite = onsite_of(labels)
    applied = vectors
    for repeat in range(2):
        extended = extended_2(applied, ((("rows", "cols"), 1),), REACH)
        applied = apply_local(extended, hopping, offsets, onsite)
    local_block = regroup(applied)
    atom_total = local_block.shape[1] * lax.axis_size("rows")
    step_count = min(3, lax.axis_size("cols") - 1)
    column_index = lax.axis_index("cols")
    for step_index in range(step_count):
        gram_matrix = (
            lax.psum(jnp.dot(local_block, local_block.T, precision=highest), "rows") / atom_total
        )
        factor = jnp.linalg.cholesky(gram_matrix)
        candidate = jax.scipy.linalg.solve_triangular(factor, local_block, lower=True)
        leader = spread(candidate, "cols", step_index)
        coupling = lax.psum(jnp.dot(leader, local_block.T, precision=highest), "rows") / atom_total
        reduced = local_block - jnp.dot(coupling.T, leader, precision=highest)
        local_block = jnp.where(
            column_index > step_index,
            reduced,
            jnp.where(column_index == step_index, leader, local_block),
        )
    return local_block


def solution(mesh):
    placed = (
        P(None, ("rows", "cols")),
        P(None, ("rows", "cols")),
        P(("rows", "cols")),
        P(None, ("rows", "cols")),
        P(None, ("rows", "cols")),
        P(None, ("rows", "cols")),
    )
    return jax.shard_map(
        on_device, mesh=mesh, in_specs=placed, out_specs=P("cols", "rows"), check_vma=False
    )
```

profile of v0, /device:TPU:2, one launch (start us, length us, event | category | flops | bytes accessed | tf_op | source)
XLA Modules:
  0.0 2041.9 jit_solution(11783422857836279491)
XLA Ops:
  7.8 1.9 collective-permute-start
  9.7 3.6 collective-permute-start.1
  15.0 3.3 collective-permute-done
  18.3 1.8 collective-permute-done.1
  21.2 30.6 %while.28 = (s32[]{:T(128)}, f32[512,256]{0,1:T(8,128)S(1)}, f32[16,256]{1,0:T(8,128)S(1)}, s32[16,256]{1,0:T(8,128)}, f32[512,768]{0,1:T(8,128)S(1)}, /*index=5*/s32[]{:T(128)}) while((s32[]{:T(128)}, f32[512,256]{0,1:T(8,128)S(1)}, f32[16,256]{1,0:T(8,128)S(1)}, s32[16,256]{1,0:T(8,128)}, f32[512,768]{0,1:T(8,128)S(1)}, ...), condition=%wide.region_1.0_spmd.clone, body=%wide.region_0.2_spmd.clone.sunk | while | flops 396290 | bytes 2635341 | solution.py:57
  51.8 3.8 collective-permute-start.2
  55.6 2.1 collective-permute-start.3
  57.8 4.8 collective-permute-done.2
  62.6 1.8 collective-permute-done.3
  65.5 30.6 %while.29 = (s32[]{:T(128)}, f32[512,256]{0,1:T(8,128)S(1)}, f32[16,256]{1,0:T(8,128)S(1)}, s32[16,256]{1,0:T(8,128)}, f32[512,768]{0,1:T(8,128)S(1)}, /*index=5*/s32[]{:T(128)}) while((s32[]{:T(128)}, f32[512,256]{0,1:T(8,128)S(1)}, f32[16,256]{1,0:T(8,128)S(1)}, s32[16,256]{1,0:T(8,128)}, f32[512,768]{0,1:T(8,128)S(1)}, ...), condition=%wide.region_3.5_spmd.clone, body=%wide.region_2.4_spmd.clone.sunk | while | flops 396290 | bytes 2635341 | solution.py:57
  97.1 21.2 %all-to-all-start = ((f32[8,64,256]{2,1,0:T(8,128)}), f32[8,64,256]{2,1,0:T(8,128)S(1)}, u32[]{:S(2)}, u32[]{:S(2)}) async-start(f32[8,64,256]{2,1,0:T(8,128)} %bitcast.1), calls=%async_computation | async-start | bytes 1048576 | tf_op jit(solution)/shard_map/all_to_all | solution.py:61
  118.3 8.9 all-to-all-done
  127.8 279.8 %psum.63 = f32[64,64]{0,1:T(8,128)S(1)} all-reduce(f32[64,64]{0,1:T(8,128)S(1)} %convolution_bitcast_fusion), channel_id=1, replica_groups=mesh['rows'=64,'cols'=8] {'rows'}, use_global_device_ids=true, to_apply=%region_4.6 | all-reduce | flops 4096 | bytes 32768 | tf_op jit(solution)/shard_map/psum | solution.py:78
  407.7 5.8 cholesky.59
  414.9 4.9 custom-call.7
  421.3 61.5 %all-reduce.4.cloned.1.call-done = f32[64,2048]{1,0:T(8,128)} async-done(((f32[64,2048]{1,0:T(8,128)}), f32[64,2048]{1,0:T(8,128)}) %all-reduce.4.cloned.1.call-update) | async-done | bytes 524304 | tf_op jit(solution)/shard_map/psum | solution.py:31
  482.9 1.6 fusion.28
  484.5 280.2 %psum.65 = f32[64,64]{0,1:T(8,128)S(1)} all-reduce(f32[64,64]{0,1:T(8,128)S(1)} %fusion.28), channel_id=1, replica_groups=mesh['rows'=64,'cols'=8] {'rows'}, use_global_device_ids=true, to_apply=%region_8.12 | all-reduce | flops 4096 | bytes 32768 | tf_op jit(solution)/shard_map/psum | solution.py:83
  764.7 1.8 fusion.8
  767.0 273.9 %psum.66 = f32[64,64]{0,1:T(8,128)S(1)} all-reduce(f32[64,64]{0,1:T(8,128)S(1)} %fusion.29), channel_id=1, replica_groups=mesh['rows'=64,'cols'=8] {'rows'}, use_global_device_ids=true, to_apply=%region_9.13 | all-reduce | flops 4096 | bytes 32768 | tf_op jit(solution)/shard_map/psum | solution.py:78
  1041.1 5.8 cholesky.70
  1048.3 4.9 custom-call.8
  1054.7 62.1 %all-reduce.6.cloned.1.call-done = f32[64,2048]{1,0:T(8,128)} async-done(((f32[64,2048]{1,0:T(8,128)}), f32[64,2048]{1,0:T(8,128)}) %all-reduce.6.cloned.1.call-update) | async-done | bytes 524304 | tf_op jit(solution)/shard_map/psum | solution.py:31
  1118.4 280.3 %psum.68 = f32[64,64]{0,1:T(8,128)S(1)} all-reduce(f32[64,64]{0,1:T(8,128)S(1)} %fusion.30), channel_id=1, replica_groups=mesh['rows'=64,'cols'=8] {'rows'}, use_global_device_ids=true, to_apply=%region_11.15 | all-reduce | flops 4096 | bytes 32768 | tf_op jit(solution)/shard_map/psum | solution.py:83
  1398.7 1.8 fusion.7
  1401.1 273.9 %psum.69 = f32[64,64]{0,1:T(8,128)S(1)} all-reduce(f32[64,64]{0,1:T(8,128)S(1)} %fusion.31), channel_id=1, replica_groups=mesh['rows'=64,'cols'=8] {'rows'}, use_global_device_ids=true, to_apply=%region_12.16 | all-reduce | flops 4096 | bytes 32768 | tf_op jit(solution)/shard_map/psum | solution.py:78
  1675.2 5.8 cholesky.81
  1682.4 4.9 custom-call.9
  1688.7 62.3 %all-reduce.8.cloned.1.call-done = f32[64,2048]{1,0:T(8,128)} async-done(((f32[64,2048]{1,0:T(8,128)}), f32[64,2048]{1,0:T(8,128)}) %all-reduce.8.cloned.1.call-update) | async-done | bytes 524304 | tf_op jit(solution)/shard_map/psum | solution.py:31
  1751.0 1.6 fusion.32
  1752.6 280.1 %psum.71 = f32[64,64]{0,1:T(8,128)S(1)} all-reduce(f32[64,64]{0,1:T(8,128)S(1)} %fusion.32), channel_id=1, replica_groups=mesh['rows'=64,'cols'=8] {'rows'}, use_global_device_ids=true, to_apply=%region_14.18 | all-reduce | flops 4096 | bytes 32768 | tf_op jit(solution)/shard_map/psum | solution.py:83
  2032.7 2.6 fusion.6
  (232 shorter events, 78.3 us)
Async XLA Ops:
  7.8 10.5 collective-permute-start
  9.7 10.3 collective-permute-start.1
  51.8 10.8 collective-permute-start.2
  55.6 8.7 collective-permute-start.3
  97.1 30.1 %all-to-all-start = ((f32[8,64,256]{2,1,0:T(8,128)}), f32[8,64,256]{2,1,0:T(8,128)S(1)}, u32[]{:S(2)}, u32[]{:S(2)}) async-start(f32[8,64,256]{2,1,0:T(8,128)} %bitcast.1), calls=%async_computation | async-start | bytes 1048576 | tf_op jit(solution)/shard_map/all_to_all | solution.py:61
  118.3 364.6 %all-reduce.4.cloned.1.call-start = ((), (), s32[]{:S(2)}) async-start(), calls=%async_computation.1 | async-start | bytes 1048576 | tf_op jit(solution)/shard_map/psum | solution.py:31
  421.3 695.5 %all-reduce.6.cloned.1.call-start = ((), (), s32[]{:S(2)}) async-start(), calls=%async_computation.2 | async-start | bytes 1048576 | tf_op jit(solution)/shard_map/psum | solution.py:31
  1054.6 696.3 %all-reduce.8.cloned.1.call-start = ((), (), s32[]{:S(2)}) async-start(), calls=%async_computation.3 | async-start | bytes 1048576 | tf_op jit(solution)/shard_map/psum | solution.py:31
Sparse Core Ops, SparseCore 0:
  421.4 61.4 all-reduce.3
  1054.8 61.9 all-reduce.5
  1688.8 62.0 all-reduce.7
where the time goes:
time: 2040 us
  blocking collectives  1670 us (82%)
  waiting for transfers between devices  206 us (10%)
  local copies, waits for them, and re-layouts  56.6 us (3%)
  other arithmetic  46.2 us (2%)
  starting transfers between devices  32.7 us (2%)
    psum x3, blocking collectives, on_device(): lax.psum(jnp.dot(leader, local_block.T, precision=highest), 'rows')  841 us
    psum x3, blocking collectives, on_device(): lax.psum(jnp.dot(local_block, local_block.T, precision=highest), 'rows')  828 us
    psum x3, waiting for transfers between devices, spread(): return lax.psum(kept, axis)  186 us
  transfers between devices with their start and end apart: 8, of which 8 were waited for; matrix products, arithmetic and copies ran while one was open for 0% of the time, Pallas kernels for 0%

commit v1 on v0

--- a/solution.py
+++ b/solution.py
@@ -80,7 +80,12 @@
         factor = jnp.linalg.cholesky(gram_matrix)
         candidate = jax.scipy.linalg.solve_triangular(factor, local_block, lower=True)
         leader = spread(candidate, "cols", step_index)
-        coupling = lax.psum(jnp.dot(leader, local_block.T, precision=highest), "rows") / atom_total
+        coupling = (
+            jnp.sum(
+                lax.all_gather(jnp.dot(leader, local_block.T, precision=highest), "rows"), axis=0
+            )
+            / atom_total
+        )
         reduced = local_block - jnp.dot(coupling.T, leader, precision=highest)
         local_block = jnp.where(
             column_index > step_index,

time: 2040 us -> 1650 us (0.81)
  blocking collectives: 1670 us -> 835 us
  waiting for transfers between devices: 206 us -> 637 us
    psum x3 -> x0, blocking collectives: 841 us -> none  [on_device(): lax.psum(jnp.dot(leader, local_block.T, precision=highest), 'rows')]
    all_gather x0 -> x3, waiting for transfers between devices: none -> 430 us  [on_device(): lax.all_gather(jnp.dot(leader, local_block.T, precision=highest), 'rows')]
  transfers between devices with their start and end apart: 8 -> 11, of which waited for: 8 -> 11; matrix products, arithmetic and copies ran while one was open for 0% -> 0% of each run, Pallas kernels for 0% -> 0%
where the time goes in v1:
time: 1650 us; the launch traced here: 1640 us
  blocking collectives  835 us (51%)
  waiting for transfers between devices  637 us (39%)
  local copies, waits for them, and re-layouts  56.8 us (3%)
  other arithmetic  51.5 us (3%)
  starting transfers between devices  33 us (2%)
    psum x3, blocking collectives, on_device(): lax.psum(jnp.dot(local_block, local_block.T, precision=highest), 'rows')  835 us
    all_gather x3, waiting for transfers between devices, on_device(): lax.all_gather(jnp.dot(leader, local_block.T, precision=highest), 'rows')  430 us
    psum x3, waiting for transfers between devices, spread(): return lax.psum(kept, axis)  187 us
  transfers between devices with their start and end apart: 11, of which 11 were waited for; matrix products, arithmetic and copies ran while one was open for 0% of the time, Pallas kernels for 0%

profile of v1, /device:TPU:2, one launch (start us, length us, event | category | flops | bytes accessed | tf_op | source)
XLA Modules:
  0.0 1643.4 jit_solution(4261758512004706428)
XLA Ops:
  7.8 1.9 collective-permute-start
  9.7 3.6 collective-permute-start.1
  15.0 3.3 collective-permute-done
  21.2 30.6 %while.28 = (s32[]{:T(128)}, f32[512,256]{0,1:T(8,128)S(1)}, f32[16,256]{1,0:T(8,128)S(1)}, s32[16,256]{1,0:T(8,128)}, f32[512,768]{0,1:T(8,128)S(1)}, /*index=5*/s32[]{:T(128)}) while((s32[]{:T(128)}, f32[512,256]{0,1:T(8,128)S(1)}, f32[16,256]{1,0:T(8,128)S(1)}, s32[16,256]{1,0:T(8,128)}, f32[512,768]{0,1:T(8,128)S(1)}, ...), condition=%wide.region_1.0_spmd.clone, body=%wide.region_0.2_spmd.clone.sunk | while | flops 396290 | bytes 2635341 | solution.py:57
  51.8 3.8 collective-permute-start.2
  55.6 2.1 collective-permute-start.3
  57.8 4.8 collective-permute-done.2
  62.6 1.8 collective-permute-done.3
  65.5 30.6 %while.29 = (s32[]{:T(128)}, f32[512,256]{0,1:T(8,128)S(1)}, f32[16,256]{1,0:T(8,128)S(1)}, s32[16,256]{1,0:T(8,128)}, f32[512,768]{0,1:T(8,128)S(1)}, /*index=5*/s32[]{:T(128)}) while((s32[]{:T(128)}, f32[512,256]{0,1:T(8,128)S(1)}, f32[16,256]{1,0:T(8,128)S(1)}, s32[16,256]{1,0:T(8,128)}, f32[512,768]{0,1:T(8,128)S(1)}, ...), condition=%wide.region_3.5_spmd.clone, body=%wide.region_2.4_spmd.clone.sunk | while | flops 396290 | bytes 2635341 | solution.py:57
  97.1 21.2 %all-to-all-start = ((f32[8,64,256]{2,1,0:T(8,128)}), f32[8,64,256]{2,1,0:T(8,128)S(1)}, u32[]{:S(2)}, u32[]{:S(2)}) async-start(f32[8,64,256]{2,1,0:T(8,128)} %bitcast.1), calls=%async_computation | async-start | bytes 1048576 | tf_op jit(solution)/shard_map/all_to_all | solution.py:61
  118.3 8.9 all-to-all-done
  127.8 279.8 %psum.42 = f32[64,64]{0,1:T(8,128)S(1)} all-reduce(f32[64,64]{0,1:T(8,128)S(1)} %convolution_bitcast_fusion), channel_id=1, replica_groups=mesh['rows'=64,'cols'=8] {'rows'}, use_global_device_ids=true, to_apply=%region_4.6 | all-reduce | flops 4096 | bytes 32768 | tf_op jit(solution)/shard_map/psum | solution.py:78
  407.7 5.8 cholesky.59
  414.9 4.9 custom-call.7
  421.3 61.6 %all-reduce.4.cloned.1.call-done = f32[64,2048]{1,0:T(8,128)} async-done(((f32[64,2048]{1,0:T(8,128)}), f32[64,2048]{1,0:T(8,128)}) %all-reduce.4.cloned.1.call-update) | async-done | bytes 524304 | tf_op jit(solution)/shard_map/psum | solution.py:31
  482.9 2.3 fusion.28
  485.3 143.5 %all-gather.7.cloned.1.call-done = f32[4096,64]{1,0:T(8,128)} async-done(((f32[64,64]{1,0:T(8,128)}), f32[4096,64]{1,0:T(8,128)}) %all-gather.7.cloned.1.call-update) | async-done | bytes 1048592 | tf_op jit(solution)/shard_map/all_gather | solution.py:85
  628.7 1.8 reduce_sum.27
  631.8 277.5 %psum.44 = f32[64,64]{0,1:T(8,128)S(1)} all-reduce(f32[64,64]{0,1:T(8,128)S(1)} %fusion.29), channel_id=1, replica_groups=mesh['rows'=64,'cols'=8] {'rows'}, use_global_device_ids=true, to_apply=%region_9.13 | all-reduce | flops 4096 | bytes 32768 | tf_op jit(solution)/shard_map/psum | solution.py:78
  909.4 5.8 cholesky.70
  916.6 4.9 custom-call.8
  923.0 62.5 %all-reduce.6.cloned.1.call-done = f32[64,2048]{1,0:T(8,128)} async-done(((f32[64,2048]{1,0:T(8,128)}), f32[64,2048]{1,0:T(8,128)}) %all-reduce.6.cloned.1.call-update) | async-done | bytes 524304 | tf_op jit(solution)/shard_map/psum | solution.py:31
  985.5 2.3 fusion.30
  988.1 142.7 %all-gather.9.cloned.1.call-done = f32[4096,64]{1,0:T(8,128)} async-done(((f32[64,64]{1,0:T(8,128)}), f32[4096,64]{1,0:T(8,128)}) %all-gather.9.cloned.1.call-update) | async-done | bytes 1048592 | tf_op jit(solution)/shard_map/all_gather | solution.py:85
  1130.8 1.8 reduce_sum.28
  1133.9 277.5 %psum.46 = f32[64,64]{0,1:T(8,128)S(1)} all-reduce(f32[64,64]{0,1:T(8,128)S(1)} %fusion.31), channel_id=1, replica_groups=mesh['rows'=64,'cols'=8] {'rows'}, use_global_device_ids=true, to_apply=%region_12.16 | all-reduce | flops 4096 | bytes 32768 | tf_op jit(solution)/shard_map/psum | solution.py:78
  1411.5 5.8 cholesky.81
  1418.6 4.9 custom-call.9
  1425.1 62.5 %all-reduce.8.cloned.1.call-done = f32[64,2048]{1,0:T(8,128)} async-done(((f32[64,2048]{1,0:T(8,128)}), f32[64,2048]{1,0:T(8,128)}) %all-reduce.8.cloned.1.call-update) | async-done | bytes 524304 | tf_op jit(solution)/shard_map/psum | solution.py:31
  1487.5 2.3 fusion.32
  1489.9 143.4 %all-gather.11.cloned.1.call-done = f32[4096,64]{1,0:T(8,128)} async-done(((f32[64,64]{1,0:T(8,128)}), f32[4096,64]{1,0:T(8,128)}) %all-gather.11.cloned.1.call-update) | async-done | bytes 1048592 | tf_op jit(solution)/shard_map/all_gather | solution.py:85
  1633.2 1.8 reduce_sum.29
  (250 shorter events, 81.7 us)
Async XLA Ops:
  7.8 10.5 collective-permute-start
  9.7 10.3 collective-permute-start.1
  51.8 10.8 collective-permute-start.2
  55.6 8.7 collective-permute-start.3
  97.1 30.1 %all-to-all-start = ((f32[8,64,256]{2,1,0:T(8,128)}), f32[8,64,256]{2,1,0:T(8,128)S(1)}, u32[]{:S(2)}, u32[]{:S(2)}) async-start(f32[8,64,256]{2,1,0:T(8,128)} %bitcast.1), calls=%async_computation | async-start | bytes 1048576 | tf_op jit(solution)/shard_map/all_to_all | solution.py:61
  118.3 364.6 %all-reduce.4.cloned.1.call-start = ((), (), s32[]{:S(2)}) async-start(), calls=%async_computation.1 | async-start | bytes 1048576 | tf_op jit(solution)/shard_map/psum | solution.py:31
  421.3 207.5 %all-gather.7.cloned.1.call-start = ((), (), s32[]{:S(2)}) async-start(), calls=%async_computation.4 | async-start | bytes 2129920 | tf_op jit(solution)/shard_map/all_gather | solution.py:85
  482.9 147.7 %copy-start = (f32[64,2048]{1,0:T(8,128)S(1)}, f32[64,2048]{1,0:T(8,128)}, u32[]{:S(2)}) copy-start(f32[64,2048]{1,0:T(8,128)} %all-reduce.4.cloned.1.call-done) | copy-start | bytes 1572868
  485.2 500.3 %all-reduce.6.cloned.1.call-start = ((), (), s32[]{:S(2)}) async-start(), calls=%async_computation.2 | async-start | bytes 1048576 | tf_op jit(solution)/shard_map/psum | solution.py:31
  922.9 207.9 %all-gather.9.cloned.1.call-start = ((), (), s32[]{:S(2)}) async-start(), calls=%async_computation.5 | async-start | bytes 2129920 | tf_op jit(solution)/shard_map/all_gather | solution.py:85
  985.5 147.1 %copy-start.1 = (f32[64,2048]{1,0:T(8,128)S(1)}, f32[64,2048]{1,0:T(8,128)}, u32[]{:S(2)}) copy-start(f32[64,2048]{1,0:T(8,128)} %all-reduce.6.cloned.1.call-done) | copy-start | bytes 1572868
  987.8 499.7 %all-reduce.8.cloned.1.call-start = ((), (), s32[]{:S(2)}) async-start(), calls=%async_computation.3 | async-start | bytes 1048576 | tf_op jit(solution)/shard_map/psum | solution.py:31
  1425.0 208.2 %all-gather.11.cloned.1.call-start = ((), (), s32[]{:S(2)}) async-start(), calls=%async_computation.6 | async-start | bytes 2129920 | tf_op jit(solution)/shard_map/all_gather | solution.py:85
  1487.5 147.6 %copy-start.2 = (f32[64,2048]{1,0:T(8,128)S(1)}, f32[64,2048]{1,0:T(8,128)}, u32[]{:S(2)}) copy-start(f32[64,2048]{1,0:T(8,128)} %all-reduce.8.cloned.1.call-done) | copy-start | bytes 1572868
Sparse Core Ops, SparseCore 0:
  421.4 61.4 all-reduce.3
  486.2 142.4 all-gather.6
  923.1 62.4 all-reduce.5
  988.3 142.4 all-gather.8
  1425.1 62.3 all-reduce.7
  1490.7 142.4 all-gather.10
